TPU v7x, 128 devices: a whole 4x4x4 slice. The times are simulated.
128 devices in a mesh: gx: 16 (over z_hi, x, core), gy: 4 (over y), gz: 2 (over z_lo).
Axes of the slice: x: 4, y: 4, z: 4 (z_hi: 2, z_lo: 2; z = z_hi * 2 + z_lo), core: 2. Of those that a mesh axis runs over, the one named last changes fastest.
Arguments:
- cells: bfloat16 [4, 64, 256, 256], P(None, 'gx', 'gy', 'gz'), may hold values from -6 to 6
- weight: bfloat16 [32, 4, 3, 3, 3], replicated, may hold values from -0.625 to 0.625
- bias: float32 [32], replicated, may hold values from -3 to 3
- cotangent: bfloat16 [32, 32, 128, 128], P(None, 'gx', 'gy', 'gz'), may hold values from -6 to 6
Outputs:
- pooled: bfloat16 [32, 32, 128, 128], P(None, 'gx', 'gy', 'gz')
- weight_grad: float32 [32, 4, 3, 3, 3], replicated
- bias_grad: float32 [32], replicated
- input_grad: float32 [4, 64, 256, 256], P(None, 'gx', 'gy', 'gz')
All inputs are finite; a program needn't handle non-finite values.
Results may differ from a plain program's by a relative error of at most 0.0029.
Values may be sent and summed in bfloat16 or wider, within the bound.
A program may use at most 128 MiB of HBM per device.

v0:
```python
import jax
import jax.numpy as jnp
from jax import lax
from jax.sharding import PartitionSpec as P

leak_slope = 0.3
soft_scale = 10.0


def extended(cells, sides, width):
    for axis, dim in sides:
        count = lax.axis_size(axis)
        head = lax.slice_in_dim(cells, 0, width, axis=dim)
        tail = lax.slice_in_dim(cells, cells.shape[dim] - width, cells.shape[dim], axis=dim)
        cells = jnp.concatenate(
            [
                lax.ppermute(tail, axis, [(i, (i + 1) % count) for i in range(count)]),
                cells,
                lax.ppermute(head, axis, [((i + 1) % count, i) for i in range(count)]),
            ],
            axis=dim,
        )
    return cells


def activate(preact):
    return leak_slope * preact + (1.0 - leak_slope) / soft_scale * jax.nn.softplus(
        soft_scale * preact
    )


def slope_of(preact):
    return leak_slope + (1.0 - leak_slope) * jax.nn.sigmoid(soft_scale * preact)


def on_device(cells, weight, bias, cotangent):
    chan_in, cells_x, cells_y, cells_z = cells.shape
    chan_out = weight.shape[0]
    stencil = [
        (shift_a, shift_b, shift_e)
        for shift_a in range(3)
        for shift_b in range(3)
        for shift_e in range(3)
    ]
    widened = extended(cells, (("gx", 1), ("gy", 2), ("gz", 3)), 1)
    patches = jnp.stack(
        [
            widened[:, sa : sa + cells_x, sb : sb + cells_y, se : se + cells_z]
            for sa, sb, se in stencil
        ],
        axis=1,
    )
    patches = patches.reshape(chan_in * 27, cells_x, cells_y, cells_z)
    weight_mat = weight.reshape(chan_out, chan_in * 27)
    preact = (
        jnp.einsum("ok,kxyz->oxyz", weight_mat, patches, preferred_element_type=jnp.float32)
        + bias[:, None, None, None]
    )
    activated = activate(preact)
    pooled = (
        activated.reshape(chan_out, cells_x // 2, 2, cells_y // 2, 2, cells_z // 2, 2)
        .mean(axis=(2, 4, 6))
        .astype(jnp.bfloat16)
    )
    spread = jnp.broadcast_to(
        cotangent.astype(jnp.float32)[:, :, None, :, None, :, None],
        (chan_out, cells_x // 2, 2, cells_y // 2, 2, cells_z // 2, 2),
    )
    spread = spread.reshape(chan_out, cells_x, cells_y, cells_z)
    delta = (slope_of(preact) * spread * 0.125).astype(jnp.bfloat16)
    weight_local = jnp.einsum("oxyz,kxyz->ok", delta, patches, preferred_element_type=jnp.float32)
    bias_local = jnp.sum(delta, axis=(1, 2, 3), dtype=jnp.float32)
    weight_total, bias_grad = lax.psum((weight_local, bias_local), ("gx", "gy", "gz"))
    weight_grad = weight_total.reshape(chan_out, chan_in, 3, 3, 3)
    delta_wide = extended(delta, (("gx", 1), ("gy", 2), ("gz", 3)), 1)
    input_grad = jnp.zeros((chan_in, cells_x, cells_y, cells_z), jnp.float32)
    for sa, sb, se in stencil:
        window = delta_wide[:, sa : sa + cells_x, sb : sb + cells_y, se : se + cells_z]
        input_grad = input_grad + jnp.einsum(
            "oc,oxyz->cxyz",
            weight[:, :, 2 - sa, 2 - sb, 2 - se],
            window,
            preferred_element_type=jnp.float32,
        )
    return (pooled, weight_grad, bias_grad, input_grad)


def solution(mesh):
    in_specs = (P(None, "gx", "gy", "gz"), P(), P(), P(None, "gx", "gy", "gz"))
    out_specs = (P(None, "gx", "gy", "gz"), P(), P(), P(None, "gx", "gy", "gz"))
    return jax.shard_map(
        on_device, mesh=mesh, in_specs=in_specs, out_specs=out_specs, check_vma=False
    )
```

profile of v0, /device:TPU:0, one launch (start us, length us, event | category | flops | bytes accessed | tf_op | source)
XLA Modules:
  0.0 232.9 jit_solution(10944951480757157942)
XLA Ops:
  1.6 5.7 %collective-permute-start.1 = (bf16[4,1,64,128]{3,2,1,0:T(8,128)(2,1)S(1)}, bf16[4,1,64,128]{3,2,1,0:T(8,128)(2,1)S(1)}, u32[]{:S(2)}, u32[]{:S(2)}) collective-permute-start(bf16[4,1,64,128]{3,2,1,0:T(8,128)(2,1)S(1)} %get-tuple-element.35), channel_id=1, source_target_pairs={{8,0},{16,8},{24,16},{32,24},{40,32},{48,40},{56,48},{64,56},{72,6... | collective-permute-start | bytes 196616 | tf_op jit(solution)/shard_map/ppermute | solution.py:19
  7.3 1.9 collective-permute-done
  10.2 3.1 %collective-permute-start.3 = (bf16[4,6,1,128]{3,2,1,0:T(2,128)(2,1)S(1)}, bf16[4,6,1,128]{3,2,1,0:T(2,128)(2,1)S(1)}, u32[]{:S(2)}, u32[]{:S(2)}) collective-permute-start(bf16[4,6,1,128]{3,2,1,0:T(2,128)(2,1)S(1)} %get-tuple-element.34), channel_id=1, source_target_pairs={{2,0},{4,2},{6,4},{0,6},{3,1},{5,3},{7,5},{1,7},{10,8},{12,10},{14... | collective-permute-start | bytes 18440 | tf_op jit(solution)/shard_map/ppermute | solution.py:19
  13.3 1.4 collective-permute-done.3
  14.7 3.5 %collective-permute-done.2 = bf16[4,6,1,128]{3,2,1,0:T(2,128)(2,1)S(1)} collective-permute-done((bf16[4,6,1,128]{3,2,1,0:T(2,128)(2,1)S(1)}, bf16[4,6,1,128]{3,2,1,0:T(2,128)(2,1)S(1)}, u32[]{:S(2)}, u32[]{:S(2)}) %collective-permute-start.2) | collective-permute-done | bytes 6176 | tf_op jit(solution)/shard_map/ppermute | solution.py:17
  18.6 1.8 collective-permute-start.5
  20.9 1.7 copy.72
  22.7 7.9 %broadcast_in_dim.2 = f32[32,2,2,32,2,64,2]{0,6,5,4,3,2,1:T(2,128)} broadcast(f32[32,2,32,64]{0,3,2,1:T(8,128)S(1)} %copy.72), dimensions={0,1,3,5} | broadcast | bytes 4718592 | tf_op jit(solution)/shard_map/broadcast_in_dim | solution.py:65
  30.5 11.4 %copy.73 = f32[32,4,64,128]{3,0,2,1:T(8,128)} copy(f32[32,4,64,128]{0,3,2,1:T(8,128)} %bitcast.435) | data formatting | bytes 8388608 | tf_op jit(solution)/shard_map/reshape | solution.py:69
  42.0 2.2 pad_maximum_fusion.3
  48.1 9.9 %convert_reduce_fusion = (f32[32]{0:T(128)S(1)}, bf16[32,4,64,128]{3,0,2,1:T(8,128)(2,1)S(1)}, f32[32,4,64,128]{3,0,2,1:T(8,128)}) fusion(f32[32,4,64,128]{3,0,2,1:T(8,128)S(1)} %copy-done.1, f32[32]{0:T(128)S(1)} %copy-done.13, bf16[32,108]{0,1:T(8,128)(2,1)S(1)} %reshape.26, bf16[108,4,64,128]{3,2,1,0:T(8,128)(2,1)S(1)} %bitcast.437), kind=kOutput, calls=%fused_computation.23 | convolution fusion | flops 248512480 | bytes 17570816 | tf_op jit(solution)/shard_map/ok,kxyz->oxyz/dot_general | solution.py:56
  57.9 6.6 %fusion.167 = f32[32,108]{0,1:T(8,128)S(1)} fusion(bf16[32,4,64,128]{3,0,2,1:T(8,128)(2,1)S(1)} %get-tuple-element.19, bf16[108,4,64,128]{3,2,1,0:T(8,128)(2,1)S(1)} %bitcast.438), kind=kOutput, calls=%fused_computation.110 | convolution fusion | flops 226492416 | bytes 9188864 | tf_op jit(solution)/shard_map/oxyz,kxyz->ok/dot_general | solution.py:71
  65.6 10.5 %copy.71 = f32[32,4,64,128]{0,3,2,1:T(8,128)} copy(f32[32,4,64,128]{3,0,2,1:T(8,128)} %get-tuple-element.20) | data formatting | bytes 8388608 | tf_op jit(solution)/shard_map/add | solution.py:27
  76.1 3.1 %collective-permute-start.7 = (bf16[32,1,64,128]{3,0,2,1:T(8,128)(2,1)}, bf16[32,1,64,128]{3,0,2,1:T(8,128)(2,1)S(1)}, u32[]{:S(2)}, u32[]{:S(2)}) collective-permute-start(bf16[32,1,64,128]{3,0,2,1:T(8,128)(2,1)} %get-tuple-element.28), channel_id=1, source_target_pairs={{8,0},{16,8},{24,16},{32,24},{40,32},{48,40},{56,48},{64,56},{72,6... | collective-permute-start | bytes 1572872 | tf_op jit(solution)/shard_map/ppermute | solution.py:19
  79.2 13.1 %reduce_sum.18 = f32[32,2,32,64]{0,3,2,1:T(8,128)} reduce(f32[32,2,2,32,2,64,2]{0,6,5,4,3,2,1:T(2,128)} %bitcast.436, f32[]{:T(128)} %constant.2.clone.1), dimensions={2,4,6}, to_apply=%region_0.1 | reduce | flops 917504 | bytes 4718596 | tf_op jit(solution)/shard_map/reduce_sum | solution.py:62
  92.3 2.9 %multiply_convert_fusion = bf16[32,2,32,64]{0,3,2,1:T(8,128)(2,1)} fusion(f32[32,2,32,64]{0,3,2,1:T(8,128)} %reduce_sum.18), kind=kLoop, calls=%fused_computation.72 | loop fusion | flops 262144 | bytes 786432 | tf_op jit(solution)/shard_map/convert_element_type | solution.py:63
  95.1 2.8 %copy.80 = bf16[32,2,32,64]{3,2,1,0:T(8,128)(2,1)} copy(bf16[32,2,32,64]{0,3,2,1:T(8,128)(2,1)} %multiply_convert_fusion) | data formatting | bytes 524288
  97.9 68.2 %all-reduce = (f32[32,4,3,3,3]{0,4,3,2,1:T(4,128)S(1)}, f32[32]{0:T(128)}) all-reduce(f32[32,4,3,3,3]{0,4,3,2,1:T(4,128)S(1)} %reshape.29, f32[32]{0:T(128)S(1)} %get-tuple-element.18), channel_id=1, replica_groups=mesh['gx'=16,'gy'=4,'gz'=2] {'gx','gy','gz'}, use_global_device_ids=true, to_apply=%region_1.2 | all-reduce | flops 3488 | bytes 27904 | tf_op jit(solution)/shard_map/psum | solution.py:73
  168.9 1.3 collective-permute-start.8
  170.2 1.2 fusion.95
  171.4 1.2 fusion.18
  172.6 1.6 collective-permute-done.8
  174.9 4.1 %fusion.271 = (bf16[32,6,66,1]{3,0,2,1:T(8,128)(2,1)}, bf16[32,6,66,1]{3,0,2,1:T(8,128)(2,1)}) fusion(bf16[32,6,66,128]{3,0,2,1:T(8,128)(2,1)S(1)} %pad_maximum_fusion.1), kind=kLoop, calls=%fused_computation.251 | loop fusion | bytes 101376 | tf_op jit(solution)/shard_map/slice | solution.py:14
  179.0 4.8 %copy.76 = bf16[32,6,66,1]{2,0,3,1:T(8,128)(2,1)S(1)} copy(bf16[32,6,66,1]{3,0,2,1:T(8,128)(2,1)} %get-tuple-element.23) | data formatting | bytes 50688 | tf_op jit(solution)/shard_map/slice | solution.py:14
  185.0 4.8 %copy.78 = bf16[32,6,66,1]{2,0,3,1:T(8,128)(2,1)S(1)} copy(bf16[32,6,66,1]{3,0,2,1:T(8,128)(2,1)} %get-tuple-element.24) | data formatting | bytes 50688 | tf_op jit(solution)/shard_map/slice | solution.py:13
  191.9 1.2 convolution_bitcast_fusion.1
  193.1 1.2 fusion.219
  196.7 1.2 fusion.238
  197.9 6.0 %copy.77 = bf16[32,6,66,1]{3,0,2,1:T(8,128)(2,1)} copy(bf16[32,6,66,1]{2,0,3,1:T(8,128)(2,1)S(1)} %collective-permute-done.10) | data formatting | bytes 50688 | tf_op jit(solution)/shard_map/ppermute | solution.py:17
  203.9 6.0 %copy.79 = bf16[32,6,66,1]{3,0,2,1:T(8,128)(2,1)} copy(bf16[32,6,66,1]{2,0,3,1:T(8,128)(2,1)S(1)} %collective-permute-done.11) | data formatting | bytes 50688 | tf_op jit(solution)/shard_map/ppermute | solution.py:19
  209.9 9.5 %maximum_maximum_fusion = (bf16[32,6,66,129]{3,0,2,1:T(8,128)(2,1)S(1)}, bf16[32,6,66,129]{3,0,2,1:T(8,128)(2,1)S(1)}) fusion(bf16[32,6,1,128]{3,0,2,1:T(8,128)(2,1)S(1)} %collective-permute-done.9, bf16[32,1,64,128]{3,0,2,1:T(8,128)(2,1)S(1)} %collective-permute-done.7, bf16[32,4,64,128]{3,0,2,1:T(8,128)(2,1)S(1)} %get-tuple-element.19, ...), kind=kLoop, calls=%fused_computation.5 | loop fusion | flops 39232512 | bytes 9833472 | tf_op jit(solution)/shard_map/concatenate | solution.py:15
  230.4 1.4 fusion.146
  (106 shorter events, 28.4 us)
Async XLA Ops:
  1.5 7.6 %collective-permute-start = (bf16[4,1,64,128]{3,2,1,0:T(8,128)(2,1)S(1)}, bf16[4,1,64,128]{3,2,1,0:T(8,128)(2,1)S(1)}, u32[]{:S(2)}, u32[]{:S(2)}) collective-permute-start(bf16[4,1,64,128]{3,2,1,0:T(8,128)(2,1)S(1)} %get-tuple-element.36), channel_id=1, source_target_pairs={{0,8},{8,16},{16,24},{24,32},{32,40},{40,48},{48,56},{56,64},{64,7... | collective-permute-start | bytes 196616 | tf_op jit(solution)/shard_map/ppermute | solution.py:17
  1.6 8.5 %collective-permute-start.1 = (bf16[4,1,64,128]{3,2,1,0:T(8,128)(2,1)S(1)}, bf16[4,1,64,128]{3,2,1,0:T(8,128)(2,1)S(1)}, u32[]{:S(2)}, u32[]{:S(2)}) collective-permute-start(bf16[4,1,64,128]{3,2,1,0:T(8,128)(2,1)S(1)} %get-tuple-element.35), channel_id=1, source_target_pairs={{8,0},{16,8},{24,16},{32,24},{40,32},{48,40},{56,48},{64,56},{72,6... | collective-permute-start | bytes 196616 | tf_op jit(solution)/shard_map/ppermute | solution.py:19
  10.2 4.5 %collective-permute-start.3 = (bf16[4,6,1,128]{3,2,1,0:T(2,128)(2,1)S(1)}, bf16[4,6,1,128]{3,2,1,0:T(2,128)(2,1)S(1)}, u32[]{:S(2)}, u32[]{:S(2)}) collective-permute-start(bf16[4,6,1,128]{3,2,1,0:T(2,128)(2,1)S(1)} %get-tuple-element.34), channel_id=1, source_target_pairs={{2,0},{4,2},{6,4},{0,6},{3,1},{5,3},{7,5},{1,7},{10,8},{12,10},{14... | collective-permute-start | bytes 18440 | tf_op jit(solution)/shard_map/ppermute | solution.py:19
  13.3 4.9 %collective-permute-start.2 = (bf16[4,6,1,128]{3,2,1,0:T(2,128)(2,1)S(1)}, bf16[4,6,1,128]{3,2,1,0:T(2,128)(2,1)S(1)}, u32[]{:S(2)}, u32[]{:S(2)}) collective-permute-start(bf16[4,6,1,128]{3,2,1,0:T(2,128)(2,1)S(1)} %get-tuple-element.33), channel_id=1, source_target_pairs={{0,2},{2,4},{4,6},{6,0},{1,3},{3,5},{5,7},{7,1},{8,10},{10,12},{12... | collective-permute-start | bytes 18440 | tf_op jit(solution)/shard_map/ppermute | solution.py:17
  18.6 23.5 %collective-permute-start.5 = (bf16[4,6,66,1]{3,2,1,0:T(8,128)(2,1)S(1)}, bf16[4,6,66,1]{3,2,1,0:T(8,128)(2,1)}, u32[]{:S(2)}, u32[]{:S(2)}) collective-permute-start(bf16[4,6,66,1]{3,2,1,0:T(8,128)(2,1)S(1)} %get-tuple-element.29), channel_id=1, source_target_pairs={{1,0},{0,1},{3,2},{2,3},{5,4},{4,5},{7,6},{6,7},{9,8},{8,9},{11,10... | collective-permute-start | bytes 9512 | tf_op jit(solution)/shard_map/ppermute | solution.py:19
  20.4 21.6 %collective-permute-start.4 = (bf16[4,6,66,1]{3,2,1,0:T(8,128)(2,1)S(1)}, bf16[4,6,66,1]{3,2,1,0:T(8,128)(2,1)}, u32[]{:S(2)}, u32[]{:S(2)}) collective-permute-start(bf16[4,6,66,1]{3,2,1,0:T(8,128)(2,1)S(1)} %get-tuple-element.30), channel_id=1, source_target_pairs={{0,1},{1,0},{2,3},{3,2},{4,5},{5,4},{6,7},{7,6},{8,9},{9,8},{10,11... | collective-permute-start | bytes 9512 | tf_op jit(solution)/shard_map/ppermute | solution.py:17
  30.5 11.4 %copy-start.11 = (bf16[32,4,3,3,3]{0,1,4,3,2:T(4,128)(2,1)S(1)}, bf16[32,4,3,3,3]{0,1,4,3,2:T(4,128)(2,1)}, u32[]{:S(2)}) copy-start(bf16[32,4,3,3,3]{0,1,4,3,2:T(4,128)(2,1)} %param.5) | copy-start | bytes 20740
  30.5 14.2 %copy-start = (bf16[4,4,64,128]{3,2,1,0:T(8,128)(2,1)S(1)}, bf16[4,4,64,128]{3,2,1,0:T(8,128)(2,1)}, u32[]{:S(2)}) copy-start(bf16[4,4,64,128]{3,2,1,0:T(8,128)(2,1)} %param.4) | copy-start | bytes 786436
  44.8 3.3 %copy-start.1 = (f32[32,4,64,128]{3,0,2,1:T(8,128)S(1)}, f32[32,4,64,128]{3,0,2,1:T(8,128)}, u32[]{:S(2)}) copy-start(f32[32,4,64,128]{3,0,2,1:T(8,128)} %copy.73) | copy-start | bytes 12582916
  44.8 3.3 %copy-start.13 = (f32[32]{0:T(128)S(1)}, f32[32]{0:T(128)}, u32[]{:S(2)}) copy-start(f32[32]{0:T(128)} %param.6) | copy-start | bytes 388
  76.1 91.8 %collective-permute-start.7 = (bf16[32,1,64,128]{3,0,2,1:T(8,128)(2,1)}, bf16[32,1,64,128]{3,0,2,1:T(8,128)(2,1)S(1)}, u32[]{:S(2)}, u32[]{:S(2)}) collective-permute-start(bf16[32,1,64,128]{3,0,2,1:T(8,128)(2,1)} %get-tuple-element.28), channel_id=1, source_target_pairs={{8,0},{16,8},{24,16},{32,24},{40,32},{48,40},{56,48},{64,56},{72,6... | collective-permute-start | bytes 1572872 | tf_op jit(solution)/shard_map/ppermute | solution.py:19
  79.2 88.7 %collective-permute-start.6 = (bf16[32,1,64,128]{3,0,2,1:T(8,128)(2,1)}, bf16[32,1,64,128]{3,0,2,1:T(8,128)(2,1)S(1)}, u32[]{:S(2)}, u32[]{:S(2)}) collective-permute-start(bf16[32,1,64,128]{3,0,2,1:T(8,128)(2,1)} %get-tuple-element.27), channel_id=1, source_target_pairs={{0,8},{8,16},{16,24},{24,32},{32,40},{40,48},{48,56},{56,64},{64,7... | collective-permute-start | bytes 1572872 | tf_op jit(solution)/shard_map/ppermute | solution.py:17
  79.2 87.6 %copy-start.12 = (bf16[32,4,3,3,3]{0,1,4,3,2:T(4,128)(2,1)S(1)}, bf16[32,4,3,3,3]{0,1,4,3,2:T(4,128)(2,1)}, u32[]{:S(2)}) copy-start(bf16[32,4,3,3,3]{0,1,4,3,2:T(4,128)(2,1)} %param.5) | copy-start | bytes 20740
  167.9 4.7 %collective-permute-start.9 = (bf16[32,6,1,128]{3,0,2,1:T(8,128)(2,1)S(1)}, bf16[32,6,1,128]{3,0,2,1:T(8,128)(2,1)S(1)}, u32[]{:S(2)}, u32[]{:S(2)}) collective-permute-start(bf16[32,6,1,128]{3,0,2,1:T(8,128)(2,1)S(1)} %get-tuple-element.26), channel_id=1, source_target_pairs={{2,0},{4,2},{6,4},{0,6},{3,1},{5,3},{7,5},{1,7},{10,8},{12,10},{14... | collective-permute-start | bytes 147464 | tf_op jit(solution)/shard_map/ppermute | solution.py:19
  168.9 5.3 %collective-permute-start.8 = (bf16[32,6,1,128]{3,0,2,1:T(8,128)(2,1)S(1)}, bf16[32,6,1,128]{3,0,2,1:T(8,128)(2,1)S(1)}, u32[]{:S(2)}, u32[]{:S(2)}) collective-permute-start(bf16[32,6,1,128]{3,0,2,1:T(8,128)(2,1)S(1)} %get-tuple-element.25), channel_id=1, source_target_pairs={{0,2},{2,4},{4,6},{6,0},{1,3},{3,5},{5,7},{7,1},{8,10},{10,12},{12... | collective-permute-start | bytes 147464 | tf_op jit(solution)/shard_map/ppermute | solution.py:17
  183.8 14.1 %collective-permute-start.10 = (bf16[32,6,66,1]{2,0,3,1:T(8,128)(2,1)S(1)}, bf16[32,6,66,1]{2,0,3,1:T(8,128)(2,1)S(1)}, u32[]{:S(2)}, u32[]{:S(2)}) collective-permute-start(bf16[32,6,66,1]{2,0,3,1:T(8,128)(2,1)S(1)} %copy.76), channel_id=1, source_target_pairs={{0,1},{1,0},{2,3},{3,2},{4,5},{5,4},{6,7},{7,6},{8,9},{9,8},{10,11... | collective-permute-start | bytes 76040 | tf_op jit(solution)/shard_map/ppermute | solution.py:17
  189.7 14.2 %collective-permute-start.11 = (bf16[32,6,66,1]{2,0,3,1:T(8,128)(2,1)S(1)}, bf16[32,6,66,1]{2,0,3,1:T(8,128)(2,1)S(1)}, u32[]{:S(2)}, u32[]{:S(2)}) collective-permute-start(bf16[32,6,66,1]{2,0,3,1:T(8,128)(2,1)S(1)} %copy.78), channel_id=1, source_target_pairs={{1,0},{0,1},{3,2},{2,3},{5,4},{4,5},{7,6},{6,7},{9,8},{8,9},{11,10... | collective-permute-start | bytes 76040 | tf_op jit(solution)/shard_map/ppermute | solution.py:19
  226.0 3.4 %copy-start.2 = (f32[4,64,128,4]{2,3,1,0:T(4,128)S(1)}, f32[4,64,128,4]{2,3,1,0:T(4,128)}, u32[]{:S(2)}) copy-start(f32[4,64,128,4]{2,3,1,0:T(4,128)} %fusion.223) | copy-start | bytes 1572868
  226.0 3.4 %copy-start.4 = (f32[4,64,128,4]{2,3,1,0:T(4,128)S(1)}, f32[4,64,128,4]{2,3,1,0:T(4,128)}, u32[]{:S(2)}) copy-start(f32[4,64,128,4]{2,3,1,0:T(4,128)} %fusion.18) | copy-start | bytes 1572868
  226.0 3.4 %copy-start.8 = (f32[4,64,128,4]{2,3,1,0:T(4,128)S(1)}, f32[4,64,128,4]{2,3,1,0:T(4,128)}, u32[]{:S(2)}) copy-start(f32[4,64,128,4]{2,3,1,0:T(4,128)} %fusion.227) | copy-start | bytes 1572868
  226.0 3.4 %copy-start.9 = (f32[4,64,128,4]{2,3,1,0:T(4,128)S(1)}, f32[4,64,128,4]{2,3,1,0:T(4,128)}, u32[]{:S(2)}) copy-start(f32[4,64,128,4]{2,3,1,0:T(4,128)} %fusion.231) | copy-start | bytes 1572868
  226.0 3.4 %copy-start.10 = (f32[4,64,128,4]{2,3,1,0:T(4,128)S(1)}, f32[4,64,128,4]{2,3,1,0:T(4,128)}, u32[]{:S(2)}) copy-start(f32[4,64,128,4]{2,3,1,0:T(4,128)} %fusion.238) | copy-start | bytes 1572868
  228.5 1.9 copy-start.3
  228.5 1.9 copy-start.5
  228.5 1.9 copy-start.6
  228.5 1.9 copy-start.7
where the time goes:
time: 236 us; the launch traced here: 233 us
  blocking collectives  68.2 us (29%)
  local copies, waits for them, and re-layouts  67.6 us (29%)
  matrix products  39.4 us (17%)
  other arithmetic  29.3 us (12%)
  starting transfers between devices  18.7 us (8%)
  waiting for transfers between devices  8.38 us (4%)
    psum x1, blocking collectives, on_device(): lax.psum((weight_local, bias_local), ('gx', 'gy', 'gz'))  68.2 us
    dot_general x27, matrix products, on_device(): jnp.einsum('oc,oxyz->cxyz', weight[:, :, 2 - sa, 2 - sb, 2 - se], window,...  22.9 us
    ppermute x6, starting transfers between devices, extended(): lax.ppermute(head, axis, [((i + 1) % count, i) for i in range(count)])  15.6 us
    reduce_sum x1, other arithmetic, on_device(): pooled = activated.reshape(chan_out, cells_x // 2, 2, cells_y // 2, 2, ce...  13.1 us
    concatenate x4, other arithmetic, extended(): jnp.concatenate([lax.ppermute(tail, axis, [(i, (i + 1) % count) for i in...  12.6 us
    reshape x1, local copies, waits for them, and re-layouts, on_device(): spread = spread.reshape(chan_out, cells_x, cells_y, cells_z)  11.4 us
    add x1, local copies, waits for them, and re-layouts, activate(): leak_slope * preact  10.5 us
    slice x4, local copies, waits for them, and re-layouts, extended(): lax.slice_in_dim(cells, cells.shape[dim] - width, cells.shape[dim], axis=...  9.99 us
  transfers between devices with their start and end apart: 12, of which 4 were waited for; matrix products, arithmetic and copies ran while one was open for 27% of the time, Pallas kernels for 0%

commit v1 on v0

--- a/solution.py
+++ b/solution.py
@@ -2,6 +2,7 @@
 import jax.numpy as jnp
 from jax import lax
 from jax.sharding import PartitionSpec as P
+from jax.lax import psum
 
 leak_slope = 0.3
 soft_scale = 10.0
@@ -70,7 +71,7 @@
     delta = (slope_of(preact) * spread * 0.125).astype(jnp.bfloat16)
     weight_local = jnp.einsum("oxyz,kxyz->ok", delta, patches, preferred_element_type=jnp.float32)
     bias_local = jnp.sum(delta, axis=(1, 2, 3), dtype=jnp.float32)
-    weight_total, bias_grad = lax.psum((weight_local, bias_local), ("gx", "gy", "gz"))
+    weight_total, bias_grad = psum(psum((weight_local, bias_local), "gx"), ("gy", "gz"))
     weight_grad = weight_total.reshape(chan_out, chan_in, 3, 3, 3)
     delta_wide = extended(delta, (("gx", 1), ("gy", 2), ("gz", 3)), 1)
     input_grad = jnp.zeros((chan_in, cells_x, cells_y, cells_z), jnp.float32)

time: 236 us -> 271 us (1.15)
  blocking collectives: 68.2 us -> 103 us
    psum x1 -> x2, blocking collectives: 68.2 us -> 103 us  [the longest x1 70.1 us: on_device(): psum((weight_local, bias_local), 'gx')]
  transfers between devices with their start and end apart: 12 -> 12, of which waited for: 4 -> 4; matrix products, arithmetic and copies ran while one was open for 27% -> 24% of each run, Pallas kernels for 0% -> 0%
where the time goes in v1:
time: 271 us; the launch traced here: 267 us
  blocking collectives  103 us (38%)
  local copies, waits for them, and re-layouts  67.6 us (25%)
  matrix products  39.5 us (15%)
  other arithmetic  29.3 us (11%)
  starting transfers between devices  18.7 us (7%)
  waiting for transfers between devices  8.14 us (3%)
    psum x1, blocking collectives, on_device(): psum((weight_local, bias_local), 'gx')  70.1 us
    psum x1, blocking collectives, on_device(): psum(psum((weight_local, bias_local), 'gx'), ('gy', 'gz'))  32.4 us
    dot_general x27, matrix products, on_device(): jnp.einsum('oc,oxyz->cxyz', weight[:, :, 2 - sa, 2 - sb, 2 - se], window,...  22.9 us
    ppermute x6, starting transfers between devices, extended(): lax.ppermute(head, axis, [((i + 1) % count, i) for i in range(count)])  15.1 us
    reduce_sum x1, other arithmetic, on_device(): pooled = activated.reshape(chan_out, cells_x // 2, 2, cells_y // 2, 2, ce...  13.1 us
    concatenate x4, other arithmetic, extended(): jnp.concatenate([lax.ppermute(tail, axis, [(i, (i + 1) % count) for i in...  12.6 us
    reshape x1, local copies, waits for them, and re-layouts, on_device(): spread = spread.reshape(chan_out, cells_x, cells_y, cells_z)  11.4 us
    add x1, local copies, waits for them, and re-layouts, activate(): leak_slope * preact  10.5 us
  transfers between devices with their start and end apart: 12, of which 4 were waited for; matrix products, arithmetic and copies ran while one was open for 24% of the time, Pallas kernels for 0%

profile of v1, /device:TPU:0, one launch (start us, length us, event | category | flops | bytes accessed | tf_op | source)
XLA Modules:
  0.0 267.2 jit_solution(14323319255518121149)
XLA Ops:
  1.6 5.7 %collective-permute-start.1 = (bf16[4,1,64,128]{3,2,1,0:T(8,128)(2,1)S(1)}, bf16[4,1,64,128]{3,2,1,0:T(8,128)(2,1)S(1)}, u32[]{:S(2)}, u32[]{:S(2)}) collective-permute-start(bf16[4,1,64,128]{3,2,1,0:T(8,128)(2,1)S(1)} %get-tuple-element.37), channel_id=1, source_target_pairs={{8,0},{16,8},{24,16},{32,24},{40,32},{48,40},{56,48},{64,56},{72,6... | collective-permute-start | bytes 196616 | tf_op jit(solution)/shard_map/ppermute | solution.py:20
  7.3 1.9 collective-permute-done
  10.2 3.1 %collective-permute-start.3 = (bf16[4,6,1,128]{3,2,1,0:T(2,128)(2,1)S(1)}, bf16[4,6,1,128]{3,2,1,0:T(2,128)(2,1)S(1)}, u32[]{:S(2)}, u32[]{:S(2)}) collective-permute-start(bf16[4,6,1,128]{3,2,1,0:T(2,128)(2,1)S(1)} %get-tuple-element.36), channel_id=1, source_target_pairs={{2,0},{4,2},{6,4},{0,6},{3,1},{5,3},{7,5},{1,7},{10,8},{12,10},{14... | collective-permute-start | bytes 18440 | tf_op jit(solution)/shard_map/ppermute | solution.py:20
  13.3 1.4 collective-permute-done.3
  14.7 3.5 %collective-permute-done.2 = bf16[4,6,1,128]{3,2,1,0:T(2,128)(2,1)S(1)} collective-permute-done((bf16[4,6,1,128]{3,2,1,0:T(2,128)(2,1)S(1)}, bf16[4,6,1,128]{3,2,1,0:T(2,128)(2,1)S(1)}, u32[]{:S(2)}, u32[]{:S(2)}) %collective-permute-start.2) | collective-permute-done | bytes 6176 | tf_op jit(solution)/shard_map/ppermute | solution.py:18
  18.6 1.8 collective-permute-start.5
  20.9 1.7 copy.72
  22.7 7.9 %broadcast_in_dim.2 = f32[32,2,2,32,2,64,2]{0,6,5,4,3,2,1:T(2,128)} broadcast(f32[32,2,32,64]{0,3,2,1:T(8,128)S(1)} %copy.72), dimensions={0,1,3,5} | broadcast | bytes 4718592 | tf_op jit(solution)/shard_map/broadcast_in_dim | solution.py:66
  30.5 11.4 %copy.73 = f32[32,4,64,128]{3,0,2,1:T(8,128)} copy(f32[32,4,64,128]{0,3,2,1:T(8,128)} %bitcast.437) | data formatting | bytes 8388608 | tf_op jit(solution)/shard_map/reshape | solution.py:70
  42.0 2.2 pad_maximum_fusion.3
  48.0 9.9 %convert_reduce_fusion = (f32[32]{0:T(128)S(1)}, bf16[32,4,64,128]{3,0,2,1:T(8,128)(2,1)S(1)}, f32[32,4,64,128]{3,0,2,1:T(8,128)}) fusion(f32[32,4,64,128]{3,0,2,1:T(8,128)S(1)} %copy-done.1, f32[32]{0:T(128)S(1)} %copy-done.13, bf16[32,108]{0,1:T(8,128)(2,1)S(1)} %reshape.26, bf16[108,4,64,128]{3,2,1,0:T(8,128)(2,1)S(1)} %bitcast.439), kind=kOutput, calls=%fused_computation.23 | convolution fusion | flops 248512480 | bytes 17570816 | tf_op jit(solution)/shard_map/ok,kxyz->oxyz/dot_general | solution.py:57
  57.9 6.8 %fusion.167 = f32[32,108]{1,0:T(8,128)S(1)} fusion(bf16[32,4,64,128]{3,0,2,1:T(8,128)(2,1)S(1)} %get-tuple-element.21, bf16[108,4,64,128]{3,2,1,0:T(8,128)(2,1)S(1)} %bitcast.440), kind=kOutput, calls=%fused_computation.110 | convolution fusion | flops 226492416 | bytes 9188864 | tf_op jit(solution)/shard_map/oxyz,kxyz->ok/dot_general | solution.py:72
  65.7 10.5 %copy.71 = f32[32,4,64,128]{0,3,2,1:T(8,128)} copy(f32[32,4,64,128]{3,0,2,1:T(8,128)} %get-tuple-element.22) | data formatting | bytes 8388608 | tf_op jit(solution)/shard_map/add | solution.py:28
  76.2 3.1 %collective-permute-start.7 = (bf16[32,1,64,128]{3,0,2,1:T(8,128)(2,1)}, bf16[32,1,64,128]{3,0,2,1:T(8,128)(2,1)S(1)}, u32[]{:S(2)}, u32[]{:S(2)}) collective-permute-start(bf16[32,1,64,128]{3,0,2,1:T(8,128)(2,1)} %get-tuple-element.30), channel_id=1, source_target_pairs={{8,0},{16,8},{24,16},{32,24},{40,32},{48,40},{56,48},{64,56},{72,6... | collective-permute-start | bytes 1572872 | tf_op jit(solution)/shard_map/ppermute | solution.py:20
  79.3 13.1 %reduce_sum.18 = f32[32,2,32,64]{0,3,2,1:T(8,128)} reduce(f32[32,2,2,32,2,64,2]{0,6,5,4,3,2,1:T(2,128)} %bitcast.438, f32[]{:T(128)} %constant.2.clone.1), dimensions={2,4,6}, to_apply=%region_0.1 | reduce | flops 917504 | bytes 4718596 | tf_op jit(solution)/shard_map/reduce_sum | solution.py:63
  92.3 2.9 %multiply_convert_fusion = bf16[32,2,32,64]{0,3,2,1:T(8,128)(2,1)} fusion(f32[32,2,32,64]{0,3,2,1:T(8,128)} %reduce_sum.18), kind=kLoop, calls=%fused_computation.72 | loop fusion | flops 262144 | bytes 786432 | tf_op jit(solution)/shard_map/convert_element_type | solution.py:64
  95.2 2.8 %copy.80 = bf16[32,2,32,64]{3,2,1,0:T(8,128)(2,1)} copy(bf16[32,2,32,64]{0,3,2,1:T(8,128)(2,1)} %multiply_convert_fusion) | data formatting | bytes 524288
  98.0 70.1 %all-reduce = (f32[32,108]{1,0:T(8,128)S(1)}, f32[32]{0:T(128)S(1)}) all-reduce(f32[32,108]{1,0:T(8,128)S(1)} %fusion.167, f32[32]{0:T(128)S(1)} %get-tuple-element.20), channel_id=1, replica_groups=mesh['gx'=16,'gy'=4,'gz'=2] {'gx'}, use_global_device_ids=true, to_apply=%region_1.2 | all-reduce | flops 3488 | bytes 27904 | tf_op jit(solution)/shard_map/psum | solution.py:74
  168.3 32.4 %all-reduce.1 = (f32[32,4,3,3,3]{0,4,3,2,1:T(4,128)S(1)}, f32[32]{0:T(128)}) all-reduce(f32[32,4,3,3,3]{0,4,3,2,1:T(4,128)S(1)} %reshape.29, f32[32]{0:T(128)S(1)} %get-tuple-element.17), channel_id=1, replica_groups=mesh['gx'=16,'gy'=4,'gz'=2] {'gy','gz'}, use_global_device_ids=true, to_apply=%region_2.3 | all-reduce | flops 3488 | bytes 27904 | tf_op jit(solution)/shard_map/psum | solution.py:74
  203.1 1.7 collective-permute-start.8
  206.0 1.2 fusion.18
  207.2 1.4 collective-permute-done.8
  209.2 4.1 %fusion.271 = (bf16[32,6,66,1]{3,0,2,1:T(8,128)(2,1)}, bf16[32,6,66,1]{3,0,2,1:T(8,128)(2,1)}) fusion(bf16[32,6,66,128]{3,0,2,1:T(8,128)(2,1)S(1)} %pad_maximum_fusion.1), kind=kLoop, calls=%fused_computation.251 | loop fusion | bytes 101376 | tf_op jit(solution)/shard_map/slice | solution.py:15
  213.4 4.8 %copy.76 = bf16[32,6,66,1]{2,0,3,1:T(8,128)(2,1)S(1)} copy(bf16[32,6,66,1]{3,0,2,1:T(8,128)(2,1)} %get-tuple-element.25) | data formatting | bytes 50688 | tf_op jit(solution)/shard_map/slice | solution.py:15
  218.1 1.3 collective-permute-start.10
  219.5 4.8 %copy.78 = bf16[32,6,66,1]{2,0,3,1:T(8,128)(2,1)S(1)} copy(bf16[32,6,66,1]{3,0,2,1:T(8,128)(2,1)} %get-tuple-element.26) | data formatting | bytes 50688 | tf_op jit(solution)/shard_map/slice | solution.py:14
  226.2 1.2 convolution_bitcast_fusion.1
  227.5 1.2 fusion.219
  232.2 6.0 %copy.77 = bf16[32,6,66,1]{3,0,2,1:T(8,128)(2,1)} copy(bf16[32,6,66,1]{2,0,3,1:T(8,128)(2,1)S(1)} %collective-permute-done.10) | data formatting | bytes 50688 | tf_op jit(solution)/shard_map/ppermute | solution.py:18
  238.3 6.0 %copy.79 = bf16[32,6,66,1]{3,0,2,1:T(8,128)(2,1)} copy(bf16[32,6,66,1]{2,0,3,1:T(8,128)(2,1)S(1)} %collective-permute-done.11) | data formatting | bytes 50688 | tf_op jit(solution)/shard_map/ppermute | solution.py:20
  244.3 9.5 %maximum_maximum_fusion = (bf16[32,6,66,129]{3,0,2,1:T(8,128)(2,1)S(1)}, bf16[32,6,66,129]{3,0,2,1:T(8,128)(2,1)S(1)}) fusion(bf16[32,6,1,128]{3,0,2,1:T(8,128)(2,1)S(1)} %collective-permute-done.9, bf16[32,1,64,128]{3,0,2,1:T(8,128)(2,1)S(1)} %collective-permute-done.7, bf16[32,4,64,128]{3,0,2,1:T(8,128)(2,1)S(1)} %get-tuple-element.21, ...), kind=kLoop, calls=%fused_computation.5 | loop fusion | flops 39232512 | bytes 9833472 | tf_op jit(solution)/shard_map/concatenate | solution.py:16
  264.7 1.4 fusion.146
  (108 shorter events, 29.1 us)
Async XLA Ops:
  1.5 7.6 %collective-permute-start = (bf16[4,1,64,128]{3,2,1,0:T(8,128)(2,1)S(1)}, bf16[4,1,64,128]{3,2,1,0:T(8,128)(2,1)S(1)}, u32[]{:S(2)}, u32[]{:S(2)}) collective-permute-start(bf16[4,1,64,128]{3,2,1,0:T(8,128)(2,1)S(1)} %get-tuple-element.38), channel_id=1, source_target_pairs={{0,8},{8,16},{16,24},{24,32},{32,40},{40,48},{48,56},{56,64},{64,7... | collective-permute-start | bytes 196616 | tf_op jit(solution)/shard_map/ppermute | solution.py:18
  1.6 8.5 %collective-permute-start.1 = (bf16[4,1,64,128]{3,2,1,0:T(8,128)(2,1)S(1)}, bf16[4,1,64,128]{3,2,1,0:T(8,128)(2,1)S(1)}, u32[]{:S(2)}, u32[]{:S(2)}) collective-permute-start(bf16[4,1,64,128]{3,2,1,0:T(8,128)(2,1)S(1)} %get-tuple-element.37), channel_id=1, source_target_pairs={{8,0},{16,8},{24,16},{32,24},{40,32},{48,40},{56,48},{64,56},{72,6... | collective-permute-start | bytes 196616 | tf_op jit(solution)/shard_map/ppermute | solution.py:20
  10.2 4.5 %collective-permute-start.3 = (bf16[4,6,1,128]{3,2,1,0:T(2,128)(2,1)S(1)}, bf16[4,6,1,128]{3,2,1,0:T(2,128)(2,1)S(1)}, u32[]{:S(2)}, u32[]{:S(2)}) collective-permute-start(bf16[4,6,1,128]{3,2,1,0:T(2,128)(2,1)S(1)} %get-tuple-element.36), channel_id=1, source_target_pairs={{2,0},{4,2},{6,4},{0,6},{3,1},{5,3},{7,5},{1,7},{10,8},{12,10},{14... | collective-permute-start | bytes 18440 | tf_op jit(solution)/shard_map/ppermute | solution.py:20
  13.3 4.9 %collective-permute-start.2 = (bf16[4,6,1,128]{3,2,1,0:T(2,128)(2,1)S(1)}, bf16[4,6,1,128]{3,2,1,0:T(2,128)(2,1)S(1)}, u32[]{:S(2)}, u32[]{:S(2)}) collective-permute-start(bf16[4,6,1,128]{3,2,1,0:T(2,128)(2,1)S(1)} %get-tuple-element.35), channel_id=1, source_target_pairs={{0,2},{2,4},{4,6},{6,0},{1,3},{3,5},{5,7},{7,1},{8,10},{10,12},{12... | collective-permute-start | bytes 18440 | tf_op jit(solution)/shard_map/ppermute | solution.py:18
  18.6 23.4 %collective-permute-start.5 = (bf16[4,6,66,1]{3,2,1,0:T(8,128)(2,1)S(1)}, bf16[4,6,66,1]{3,2,1,0:T(8,128)(2,1)}, u32[]{:S(2)}, u32[]{:S(2)}) collective-permute-start(bf16[4,6,66,1]{3,2,1,0:T(8,128)(2,1)S(1)} %get-tuple-element.31), channel_id=1, source_target_pairs={{1,0},{0,1},{3,2},{2,3},{5,4},{4,5},{7,6},{6,7},{9,8},{8,9},{11,10... | collective-permute-start | bytes 9512 | tf_op jit(solution)/shard_map/ppermute | solution.py:20
  20.4 21.6 %collective-permute-start.4 = (bf16[4,6,66,1]{3,2,1,0:T(8,128)(2,1)S(1)}, bf16[4,6,66,1]{3,2,1,0:T(8,128)(2,1)}, u32[]{:S(2)}, u32[]{:S(2)}) collective-permute-start(bf16[4,6,66,1]{3,2,1,0:T(8,128)(2,1)S(1)} %get-tuple-element.32), channel_id=1, source_target_pairs={{0,1},{1,0},{2,3},{3,2},{4,5},{5,4},{6,7},{7,6},{8,9},{9,8},{10,11... | collective-permute-start | bytes 9512 | tf_op jit(solution)/shard_map/ppermute | solution.py:18
  30.5 11.4 %copy-start.11 = (bf16[32,4,3,3,3]{0,1,4,3,2:T(4,128)(2,1)S(1)}, bf16[32,4,3,3,3]{0,1,4,3,2:T(4,128)(2,1)}, u32[]{:S(2)}) copy-start(bf16[32,4,3,3,3]{0,1,4,3,2:T(4,128)(2,1)} %param.5) | copy-start | bytes 20740
  30.5 14.2 %copy-start = (bf16[4,4,64,128]{3,2,1,0:T(8,128)(2,1)S(1)}, bf16[4,4,64,128]{3,2,1,0:T(8,128)(2,1)}, u32[]{:S(2)}) copy-start(bf16[4,4,64,128]{3,2,1,0:T(8,128)(2,1)} %param.4) | copy-start | bytes 786436
  44.8 3.3 %copy-start.1 = (f32[32,4,64,128]{3,0,2,1:T(8,128)S(1)}, f32[32,4,64,128]{3,0,2,1:T(8,128)}, u32[]{:S(2)}) copy-start(f32[32,4,64,128]{3,0,2,1:T(8,128)} %copy.73) | copy-start | bytes 12582916
  44.8 3.3 %copy-start.13 = (f32[32]{0:T(128)S(1)}, f32[32]{0:T(128)}, u32[]{:S(2)}) copy-start(f32[32]{0:T(128)} %param.6) | copy-start | bytes 388
  76.2 126.3 %collective-permute-start.7 = (bf16[32,1,64,128]{3,0,2,1:T(8,128)(2,1)}, bf16[32,1,64,128]{3,0,2,1:T(8,128)(2,1)S(1)}, u32[]{:S(2)}, u32[]{:S(2)}) collective-permute-start(bf16[32,1,64,128]{3,0,2,1:T(8,128)(2,1)} %get-tuple-element.30), channel_id=1, source_target_pairs={{8,0},{16,8},{24,16},{32,24},{40,32},{48,40},{56,48},{64,56},{72,6... | collective-permute-start | bytes 1572872 | tf_op jit(solution)/shard_map/ppermute | solution.py:20
  79.3 123.2 %collective-permute-start.6 = (bf16[32,1,64,128]{3,0,2,1:T(8,128)(2,1)}, bf16[32,1,64,128]{3,0,2,1:T(8,128)(2,1)S(1)}, u32[]{:S(2)}, u32[]{:S(2)}) collective-permute-start(bf16[32,1,64,128]{3,0,2,1:T(8,128)(2,1)} %get-tuple-element.29), channel_id=1, source_target_pairs={{0,8},{8,16},{16,24},{24,32},{32,40},{40,48},{48,56},{56,64},{64,7... | collective-permute-start | bytes 1572872 | tf_op jit(solution)/shard_map/ppermute | solution.py:18
  79.3 122.1 %copy-start.12 = (bf16[32,4,3,3,3]{0,1,4,3,2:T(4,128)(2,1)S(1)}, bf16[32,4,3,3,3]{0,1,4,3,2:T(4,128)(2,1)}, u32[]{:S(2)}) copy-start(bf16[32,4,3,3,3]{0,1,4,3,2:T(4,128)(2,1)} %param.5) | copy-start | bytes 20740
  202.5 4.7 %collective-permute-start.9 = (bf16[32,6,1,128]{3,0,2,1:T(8,128)(2,1)S(1)}, bf16[32,6,1,128]{3,0,2,1:T(8,128)(2,1)S(1)}, u32[]{:S(2)}, u32[]{:S(2)}) collective-permute-start(bf16[32,6,1,128]{3,0,2,1:T(8,128)(2,1)S(1)} %get-tuple-element.28), channel_id=1, source_target_pairs={{2,0},{4,2},{6,4},{0,6},{3,1},{5,3},{7,5},{1,7},{10,8},{12,10},{14... | collective-permute-start | bytes 147464 | tf_op jit(solution)/shard_map/ppermute | solution.py:20
  203.1 5.5 %collective-permute-start.8 = (bf16[32,6,1,128]{3,0,2,1:T(8,128)(2,1)S(1)}, bf16[32,6,1,128]{3,0,2,1:T(8,128)(2,1)S(1)}, u32[]{:S(2)}, u32[]{:S(2)}) collective-permute-start(bf16[32,6,1,128]{3,0,2,1:T(8,128)(2,1)S(1)} %get-tuple-element.27), channel_id=1, source_target_pairs={{0,2},{2,4},{4,6},{6,0},{1,3},{3,5},{5,7},{7,1},{8,10},{10,12},{12... | collective-permute-start | bytes 147464 | tf_op jit(solution)/shard_map/ppermute | solution.py:18
  218.1 14.1 %collective-permute-start.10 = (bf16[32,6,66,1]{2,0,3,1:T(8,128)(2,1)S(1)}, bf16[32,6,66,1]{2,0,3,1:T(8,128)(2,1)S(1)}, u32[]{:S(2)}, u32[]{:S(2)}) collective-permute-start(bf16[32,6,66,1]{2,0,3,1:T(8,128)(2,1)S(1)} %copy.76), channel_id=1, source_target_pairs={{0,1},{1,0},{2,3},{3,2},{4,5},{5,4},{6,7},{7,6},{8,9},{9,8},{10,11... | collective-permute-start | bytes 76040 | tf_op jit(solution)/shard_map/ppermute | solution.py:18
  224.2 14.0 %collective-permute-start.11 = (bf16[32,6,66,1]{2,0,3,1:T(8,128)(2,1)S(1)}, bf16[32,6,66,1]{2,0,3,1:T(8,128)(2,1)S(1)}, u32[]{:S(2)}, u32[]{:S(2)}) collective-permute-start(bf16[32,6,66,1]{2,0,3,1:T(8,128)(2,1)S(1)} %copy.78), channel_id=1, source_target_pairs={{1,0},{0,1},{3,2},{2,3},{5,4},{4,5},{7,6},{6,7},{9,8},{8,9},{11,10... | collective-permute-start | bytes 76040 | tf_op jit(solution)/shard_map/ppermute | solution.py:20
  260.3 3.4 %copy-start.2 = (f32[4,64,128,4]{2,3,1,0:T(4,128)S(1)}, f32[4,64,128,4]{2,3,1,0:T(4,128)}, u32[]{:S(2)}) copy-start(f32[4,64,128,4]{2,3,1,0:T(4,128)} %fusion.223) | copy-start | bytes 1572868
  260.3 3.4 %copy-start.4 = (f32[4,64,128,4]{2,3,1,0:T(4,128)S(1)}, f32[4,64,128,4]{2,3,1,0:T(4,128)}, u32[]{:S(2)}) copy-start(f32[4,64,128,4]{2,3,1,0:T(4,128)} %fusion.18) | copy-start | bytes 1572868
  260.4 3.4 %copy-start.8 = (f32[4,64,128,4]{2,3,1,0:T(4,128)S(1)}, f32[4,64,128,4]{2,3,1,0:T(4,128)}, u32[]{:S(2)}) copy-start(f32[4,64,128,4]{2,3,1,0:T(4,128)} %fusion.227) | copy-start | bytes 1572868
  260.4 3.4 %copy-start.9 = (f32[4,64,128,4]{2,3,1,0:T(4,128)S(1)}, f32[4,64,128,4]{2,3,1,0:T(4,128)}, u32[]{:S(2)}) copy-start(f32[4,64,128,4]{2,3,1,0:T(4,128)} %fusion.231) | copy-start | bytes 1572868
  260.4 3.4 %copy-start.10 = (f32[4,64,128,4]{2,3,1,0:T(4,128)S(1)}, f32[4,64,128,4]{2,3,1,0:T(4,128)}, u32[]{:S(2)}) copy-start(f32[4,64,128,4]{2,3,1,0:T(4,128)} %fusion.238) | copy-start | bytes 1572868
  262.8 1.9 copy-start.3
  262.8 1.9 copy-start.5
  262.9 1.9 copy-start.6
  262.9 1.9 copy-start.7
